TPU v7x, 32 devices: a whole 2x2x4 slice. The times are simulated.
32 devices in a mesh: fsdp: 4 (over y, x), ctx: 4 (over z), tp: 2 (over core).
Axes of the slice: x: 2, y: 2, z: 4, core: 2. Of those that a mesh axis runs over, the one named last changes fastest.
Arguments:
- tokens: bfloat16 [8, 1024, 2048], P('fsdp', 'ctx'), may hold values from -6 to 6
- cotangent: bfloat16 [8, 1024, 2048], P('fsdp', 'ctx'), may hold values from -6 to 6
- prefix_len: int32 [8], P('fsdp'), may hold values from 102 to 512
- group_order: int32 [8], replicated, may hold values from 0 to 7, each once
- ln_gain: bfloat16 [2048], replicated, may hold values from 0.25 to 1.75
- ln_bias: bfloat16 [2048], replicated, may hold values from -4 to 4
- query_weight: bfloat16 [2048, 2048], P('fsdp', 'tp'), may hold values from -0.125 to 0.125
- query_bias: bfloat16 [2048], P('tp'), may hold values from -4 to 4
- key_weight: bfloat16 [2048, 2048], P('fsdp', 'tp'), may hold values from -0.125 to 0.125
- key_bias: bfloat16 [2048], P('tp'), may hold values from -4 to 4
- value_weight: bfloat16 [2048, 2048], P('fsdp', 'tp'), may hold values from -0.125 to 0.125
- value_bias: bfloat16 [2048], P('tp'), may hold values from -4 to 4
- out_weight: bfloat16 [2048, 2048], P('fsdp', 'tp'), may hold values from -1 to 1
- out_bias: bfloat16 [2048], replicated, may hold values from -4 to 4
- up_weight: bfloat16 [2048, 8192], P('fsdp', 'tp'), may hold values from -0.125 to 0.125
- up_bias: bfloat16 [8192], P('tp'), may hold values from -4 to 4
- down_weight: bfloat16 [2048, 8192], P('fsdp', 'tp'), may hold values from -0.0625 to 0.0625
- down_bias: bfloat16 [2048], replicated, may hold values from -4 to 4
Outputs:
- output: bfloat16 [8, 1024, 2048], P('fsdp', 'ctx')
- input_grad: bfloat16 [8, 1024, 2048], P('fsdp', 'ctx')
- ln_gain_grad: float32 [2048], replicated
- ln_bias_grad: float32 [2048], replicated
- query_weight_grad: float32 [2048, 2048], P('fsdp', 'tp')
- query_bias_grad: float32 [2048], P('tp')
- key_weight_grad: float32 [2048, 2048], P('fsdp', 'tp')
- key_bias_grad: float32 [2048], P('tp')
- value_weight_grad: float32 [2048, 2048], P('fsdp', 'tp')
- value_bias_grad: float32 [2048], P('tp')
- out_weight_grad: float32 [2048, 2048], P('fsdp', 'tp')
- up_weight_grad: float32 [2048, 8192], P('fsdp', 'tp')
- up_bias_grad: float32 [8192], P('tp')
- down_weight_grad: float32 [2048, 8192], P('fsdp', 'tp')
- out_biases_grad: float32 [2048], replicated
Inputs may be any that keep to these rules, and one draw needn't show every extreme that they name: Each number of 0 to 7 appears once; storage rows k * 128 to k * 128 + 127 of every sequence hold positions group_order[k] * 128 onwards.
All inputs are finite; a program needn't handle non-finite values.
Results may differ from a plain program's by a relative error of at most 0.012.
Values may be sent and summed in bfloat16 or wider, within the bound.
No kernel may reach another device: no remote copies, remote signals or barrier semaphores. Data moves between devices by JAX's collectives and lax.ppermute only.
A program may use at most 448 MiB of HBM per device.

v0:
```python
import jax
import jax.numpy as jnp
from jax import lax
from jax.sharding import PartitionSpec as P

HD = 64
ROT = 32
SEQ_LEN = 1024
masked_fill = -1e30
norm_eps = 1e-05


def positions(group_order, row_start, row_count, group_len):
    row_index = row_start + jnp.arange(row_count, dtype=jnp.int32)
    slot_index = row_index // group_len
    offset = row_index - slot_index * group_len
    matches = slot_index[:, None] == jnp.arange(group_order.shape[0], dtype=jnp.int32)[None, :]
    anchor = jnp.sum(jnp.where(matches, group_order[None, :], 0), axis=1)
    return anchor * group_len + offset


def rotary_tables(places):
    half_rot = ROT // 2
    frequency = jnp.power(10000.0, -2.0 * jnp.arange(half_rot, dtype=jnp.float32) / ROT)
    angles = places.astype(jnp.float32)[:, None] * frequency[None, :]
    return (jnp.cos(angles), jnp.sin(angles))


def rotate(tensor, cosine, sine_vals):
    half_rot = cosine.shape[-1]
    front_part = tensor[..., :half_rot]
    back_part = tensor[..., half_rot : 2 * half_rot]
    rest_part = tensor[..., 2 * half_rot :]
    cosine_rows = cosine[:, None, :]
    sine_rows = sine_vals[:, None, :]
    return jnp.concatenate(
        [
            front_part * cosine_rows - back_part * sine_rows,
            back_part * cosine_rows + front_part * sine_rows,
            rest_part,
        ],
        axis=-1,
    )


def gelu_tanh(values_in):
    return jax.nn.gelu(values_in, approximate=True)


def local(
    tokens,
    cotangent,
    prefix_len,
    group_order,
    ln_gain,
    ln_bias,
    query_weight,
    query_bias,
    key_weight,
    key_bias,
    value_weight,
    value_bias,
    out_weight,
    out_bias,
    up_weight,
    up_bias,
    down_weight,
    down_bias,
):
    seq_count, local_rows, model_width = tokens.shape
    token_count = seq_count * local_rows
    inner_width = query_weight.shape[1]
    local_heads = inner_width // HD
    hidden_units = up_weight.shape[1]
    group_len = SEQ_LEN // group_order.shape[0]
    score_scale = HD ** (-0.5)
    own_place = positions(group_order, lax.axis_index("ctx") * local_rows, local_rows, group_len)
    key_place = positions(group_order, 0, SEQ_LEN, group_len)
    cosine, sine_vals = rotary_tables(own_place)
    allowed = (key_place[None, None, None, :] <= own_place[None, None, :, None]) | (
        key_place[None, None, None, :] < prefix_len[:, None, None, None]
    )
    gathered = (
        lax.all_gather(query_weight, "fsdp", axis=0, tiled=True),
        lax.all_gather(key_weight, "fsdp", axis=0, tiled=True),
        lax.all_gather(value_weight, "fsdp", axis=0, tiled=True),
        lax.all_gather(out_weight, "fsdp", axis=0, tiled=True),
        lax.all_gather(up_weight, "fsdp", axis=0, tiled=True),
        lax.all_gather(down_weight, "fsdp", axis=0, tiled=True),
    )
    w_query, w_key, w_value, w_out, w_up, w_down = gathered
    inputs = tokens.reshape(token_count, model_width).astype(jnp.float32)
    centre = jnp.mean(inputs, axis=-1, keepdims=True)
    centred = inputs - centre
    inv_std = lax.rsqrt(jnp.mean(centred * centred, axis=-1, keepdims=True) + norm_eps)
    normed = centred * inv_std
    norm_gain = ln_gain.astype(jnp.float32)
    hidden = (normed * norm_gain + ln_bias.astype(jnp.float32)).astype(jnp.bfloat16)

    def project(weight, bias_vec):
        return jnp.dot(hidden, weight, preferred_element_type=jnp.float32) + bias_vec.astype(
            jnp.float32
        )

    query_rot = rotate(
        project(w_query, query_bias).reshape(seq_count, local_rows, local_heads, HD),
        cosine,
        sine_vals,
    ).astype(jnp.bfloat16)
    key_rot = (
        rotate(
            project(w_key, key_bias).reshape(seq_count, local_rows, local_heads, HD),
            cosine,
            sine_vals,
        )
        .astype(jnp.bfloat16)
        .reshape(seq_count, local_rows, inner_width)
    )
    value_rows = (
        project(w_value, value_bias)
        .astype(jnp.bfloat16)
        .reshape(seq_count, local_rows, inner_width)
    )
    keys_all, values_all = (
        lax.all_gather(key_rot, "ctx", axis=1, tiled=True),
        lax.all_gather(value_rows, "ctx", axis=1, tiled=True),
    )

    def scores_for(key_block):
        key_heads = key_block.reshape(seq_count, key_block.shape[1], local_heads, HD)
        raw_scores = (
            jnp.einsum("bqhd,bkhd->bhqk", query_rot, key_heads, preferred_element_type=jnp.float32)
            * score_scale
        )
        return jnp.where(allowed, raw_scores, masked_fill)

    masked = scores_for(keys_all)
    row_max = jnp.max(masked, axis=-1, keepdims=True)
    exponent = jnp.exp(masked - row_max)
    row_total = jnp.sum(exponent, axis=-1, keepdims=True)
    attn_probs = (exponent / row_total).astype(jnp.bfloat16)
    log_total = row_max + jnp.log(row_total)
    value_heads = values_all.reshape(seq_count, values_all.shape[1], local_heads, HD)
    context = jnp.einsum(
        "bhqk,bkhd->bqhd", attn_probs, value_heads, preferred_element_type=jnp.float32
    )
    context = context.reshape(token_count, inner_width).astype(jnp.bfloat16)
    up_proj = project(w_up, up_bias)
    activated = gelu_tanh(up_proj).astype(jnp.bfloat16)
    partial_out = jnp.dot(context, w_out.T, preferred_element_type=jnp.float32) + jnp.dot(
        activated, w_down.T, preferred_element_type=jnp.float32
    )
    branches = lax.psum(partial_out, "tp")
    output = inputs + branches + out_bias.astype(jnp.float32) + down_bias.astype(jnp.float32)
    output = output.astype(jnp.bfloat16).reshape(seq_count, local_rows, model_width)
    back_query, back_key, back_value, back_out, back_up, back_down = (
        lax.all_gather(query_weight, "fsdp", axis=0, tiled=True),
        lax.all_gather(key_weight, "fsdp", axis=0, tiled=True),
        lax.all_gather(value_weight, "fsdp", axis=0, tiled=True),
        lax.all_gather(out_weight, "fsdp", axis=0, tiled=True),
        lax.all_gather(up_weight, "fsdp", axis=0, tiled=True),
        lax.all_gather(down_weight, "fsdp", axis=0, tiled=True),
    )
    keys_back, values_back = (
        lax.all_gather(key_rot, "ctx", axis=1, tiled=True),
        lax.all_gather(value_rows, "ctx", axis=1, tiled=True),
    )
    grad_out = cotangent.reshape(token_count, model_width)
    grad_context = jnp.dot(grad_out, back_out, preferred_element_type=jnp.float32).astype(
        jnp.bfloat16
    )
    grad_heads = grad_context.reshape(seq_count, local_rows, local_heads, HD)
    key_heads_back = keys_back.reshape(seq_count, keys_back.shape[1], local_heads, HD)
    value_heads_back = values_back.reshape(seq_count, values_back.shape[1], local_heads, HD)
    probs_back = jnp.exp(scores_for(keys_back) - log_total)
    grad_probs = jnp.einsum(
        "bqhd,bkhd->bhqk", grad_heads, value_heads_back, preferred_element_type=jnp.float32
    )
    row_delta = jnp.sum(probs_back * grad_probs, axis=-1, keepdims=True)
    grad_scores = (probs_back * (grad_probs - row_delta)).astype(jnp.bfloat16)
    probs_low = probs_back.astype(jnp.bfloat16)
    grad_query_rot = (
        jnp.einsum(
            "bhqk,bkhd->bqhd", grad_scores, key_heads_back, preferred_element_type=jnp.float32
        )
        * score_scale
    )
    row_count = local_rows * lax.axis_size("ctx")
    grad_key_part = (
        jnp.einsum("bhqk,bqhd->kbhd", grad_scores, query_rot, preferred_element_type=jnp.float32)
        * score_scale
    )
    grad_value_part = jnp.einsum(
        "bhqk,bqhd->kbhd", probs_low, grad_heads, preferred_element_type=jnp.float32
    )
    key_grads = lax.psum_scatter(
        jnp.concatenate(
            [
                grad_key_part.reshape(row_count, seq_count, inner_width),
                grad_value_part.reshape(row_count, seq_count, inner_width),
            ],
            axis=2,
        ),
        "ctx",
        scatter_dimension=0,
        tiled=True,
    )
    key_grads = jnp.transpose(key_grads, (1, 0, 2))
    key_grad_rot = key_grads[:, :, :inner_width].reshape(seq_count, local_rows, local_heads, HD)
    grad_value = (
        key_grads[:, :, inner_width:].astype(jnp.bfloat16).reshape(token_count, inner_width)
    )
    grad_query = (
        rotate(grad_query_rot, cosine, -sine_vals)
        .astype(jnp.bfloat16)
        .reshape(token_count, inner_width)
    )
    grad_key = (
        rotate(key_grad_rot, cosine, -sine_vals)
        .astype(jnp.bfloat16)
        .reshape(token_count, inner_width)
    )
    grad_activated = jnp.dot(grad_out, back_down, preferred_element_type=jnp.float32)
    gelu_pull = jax.vjp(gelu_tanh, up_proj)[1]
    grad_up = gelu_pull(grad_activated)[0].astype(jnp.bfloat16)
    partial_hidden = (
        jnp.dot(grad_query, back_query.T, preferred_element_type=jnp.float32)
        + jnp.dot(grad_key, back_key.T, preferred_element_type=jnp.float32)
        + jnp.dot(grad_value, back_value.T, preferred_element_type=jnp.float32)
        + jnp.dot(grad_up, back_up.T, preferred_element_type=jnp.float32)
    )
    grad_hidden = lax.psum(partial_hidden, "tp")
    grad_scaled = grad_hidden * norm_gain
    grad_normed = inv_std * (
        grad_scaled
        - jnp.mean(grad_scaled, axis=-1, keepdims=True)
        - normed * jnp.mean(grad_scaled * normed, axis=-1, keepdims=True)
    )
    grad_float = grad_out.astype(jnp.float32)
    input_grad = (
        (grad_float + grad_normed).astype(jnp.bfloat16).reshape(seq_count, local_rows, model_width)
    )
    small_terms = (
        jnp.sum(grad_hidden * normed, axis=0),
        jnp.sum(grad_hidden, axis=0),
        jnp.sum(grad_query, axis=0, dtype=jnp.float32),
        jnp.sum(grad_key, axis=0, dtype=jnp.float32),
        jnp.sum(grad_value, axis=0, dtype=jnp.float32),
        jnp.sum(grad_up, axis=0, dtype=jnp.float32),
        jnp.sum(grad_float, axis=0),
    )
    gain_grad, shift_grad, qbias_grad, kbias_grad, vbias_grad, ubias_grad, obias_grad = lax.psum(
        (
            small_terms[0],
            small_terms[1],
            small_terms[2],
            small_terms[3],
            small_terms[4],
            small_terms[5],
            small_terms[6],
        ),
        ("fsdp", "ctx"),
    )
    grads_in = jnp.concatenate([grad_query, grad_key, grad_value, grad_up], axis=1)
    acts_out = jnp.concatenate([context, activated], axis=1)
    left_part = jnp.einsum("tc,tn->cn", hidden, grads_in, preferred_element_type=jnp.float32)
    right_part = jnp.einsum("tc,tn->cn", grad_out, acts_out, preferred_element_type=jnp.float32)
    scattered = lax.psum_scatter(
        jnp.concatenate([left_part, right_part], axis=1), "fsdp", scatter_dimension=0, tiled=True
    )
    weight_grads = lax.psum(scattered, "ctx")
    edge_two = 2 * inner_width
    edge_three = 3 * inner_width
    edge_four = edge_three + hidden_units
    edge_five = edge_four + inner_width
    return (
        output,
        input_grad,
        gain_grad,
        shift_grad,
        weight_grads[:, :inner_width],
        qbias_grad,
        weight_grads[:, inner_width:edge_two],
        kbias_grad,
        weight_grads[:, edge_two:edge_three],
        vbias_grad,
        weight_grads[:, edge_four:edge_five],
        weight_grads[:, edge_three:edge_four],
        ubias_grad,
        weight_grads[:, edge_five:],
        obias_grad,
    )


def solution(mesh):
    return jax.shard_map(
        local,
        mesh=mesh,
        in_specs=(
            P("fsdp", "ctx", None),
            P("fsdp", "ctx", None),
            P("fsdp"),
            P(),
            P(),
            P(),
            P("fsdp", "tp"),
            P("tp"),
            P("fsdp", "tp"),
            P("tp"),
            P("fsdp", "tp"),
            P("tp"),
            P("fsdp", "tp"),
            P(),
            P("fsdp", "tp"),
            P("tp"),
            P("fsdp", "tp"),
            P(),
        ),
        out_specs=(
            P("fsdp", "ctx", None),
            P("fsdp", "ctx", None),
            P(),
            P(),
            P("fsdp", "tp"),
            P("tp"),
            P("fsdp", "tp"),
            P("tp"),
            P("fsdp", "tp"),
            P("tp"),
            P("fsdp", "tp"),
            P("fsdp", "tp"),
            P("tp"),
            P("fsdp", "tp"),
            P(),
        ),
        check_vma=False,
    )
```

profile of v0, /device:TPU:0, one launch (start us, length us, event | category | flops | bytes accessed | tf_op | source)
XLA Modules:
  0.0 2836.2 jit_solution(8669938643243681293)
XLA Ops:
  11.8 2.2 fusion.32
  14.0 51.3 %all-gather.9.cloned.1.call-done = bf16[2048,1024]{1,0:T(8,128)(2,1)} async-done(((bf16[512,1024]{1,0:T(8,128)(2,1)}), bf16[2048,1024]{1,0:T(8,128)(2,1)}) %all-gather.9.cloned.1.call-update) | async-done | bytes 4194320 | tf_op jit(solution)/shard_map/all_gather | solution.py:86
  65.3 6.1 add_convert_fusion
  72.7 47.3 %all-gather.15.cloned.1.call-done = bf16[2048,1024]{1,0:T(8,128)(2,1)} async-done(((bf16[512,1024]{1,0:T(8,128)(2,1)}), bf16[2048,1024]{1,0:T(8,128)(2,1)}) %all-gather.15.cloned.1.call-update) | async-done | bytes 4194320 | tf_op jit(solution)/shard_map/all_gather | solution.py:85
  119.9 5.8 convolution_add_fusion.1
  125.8 2.9 copy.73
  128.6 3.7 reshape.388
  132.3 2.5 slice.114
  134.8 39.8 %all-gather.13.cloned.1.call-done = bf16[2048,1024]{1,0:T(8,128)(2,1)} async-done(((bf16[512,1024]{1,0:T(8,128)(2,1)}), bf16[2048,1024]{1,0:T(8,128)(2,1)}) %all-gather.13.cloned.1.call-update) | async-done | bytes 4194320 | tf_op jit(solution)/shard_map/all_gather | solution.py:84
  174.5 5.8 convolution_add_fusion.2
  180.3 4.5 reshape.399
  184.9 8.3 fusion.57
  193.2 3.6 copy.98
  196.8 3.5 copy.97
  202.3 1.5 pad_maximum_fusion.3
  207.9 2.8 slice.85
  210.7 18.2 all-gather.19.cloned.1.call-done
  228.9 5.2 convolution_convert_fusion
  234.1 2.7 reshape.400
  236.8 2.9 copy.81
  239.7 2.4 copy.99
  242.1 69.7 %all-gather.11.cloned.1.call-done = bf16[2,1024,1024]{2,1,0:T(8,128)(2,1)} async-done(((bf16[2,256,1024]{2,1,0:T(8,128)(2,1)}), bf16[2,1024,1024]{2,1,0:T(8,128)(2,1)}) %all-gather.11.cloned.1.call-update) | async-done | bytes 4194320 | tf_op jit(solution)/shard_map/all_gather | solution.py:126
  311.7 6.2 copy.68
  318.0 74.9 %all-gather.17.cloned.1.call-done = bf16[2,1024,1024]{1,2,0:T(8,128)(2,1)} async-done(((bf16[2,256,1024]{1,2,0:T(8,128)(2,1)}), bf16[2,1024,1024]{1,2,0:T(8,128)(2,1)}) %all-gather.17.cloned.1.call-update) | async-done | bytes 4194320 | tf_op jit(solution)/shard_map/all_gather | solution.py:125
  392.9 20.1 fusion.59
  412.9 14.6 fusion
  427.5 22.3 multiply_reduce_fusion
  449.8 29.6 %multiply_convert_fusion = bf16[2,16,256,1024]{3,2,1,0:T(8,128)(2,1)} fusion(f32[2,16,256,1024]{3,2,1,0:T(8,128)} %get-tuple-element.72, f32[2,16,256,1024]{3,2,1,0:T(8,128)} %get-tuple-element.70, f32[2,16,256]{2,1,0:T(8,128)S(1)} %get-tuple-element.71, f32[2,16,256]{2,1,0:T(8,128)S(1)} %log_add_fusion), kind=kLoop, calls=%fused_computation.1 | loop fusion | flops 33554432 | bytes 83951616 | tf_op jit(solution)/shard_map/convert_element_type | solution.py:180
  479.4 12.2 broadcast_multiply_fusion
  491.6 17.0 fusion.2
  508.6 11.9 pad_maximum_fusion.1
  521.2 15.1 fusion.43
  538.6 1.3 copy.88
  539.9 13.7 multiply_bitcast_fusion
  553.6 1.3 slice.91
  554.9 14.4 fusion.61
  569.3 140.3 %all-gather.23.cloned.1.call-done = bf16[2048,4096]{1,0:T(8,128)(2,1)} async-done(((bf16[512,4096]{1,0:T(8,128)(2,1)}), bf16[2048,4096]{1,0:T(8,128)(2,1)}) %all-gather.23.cloned.1.call-update) | async-done | bytes 16777232 | tf_op jit(solution)/shard_map/all_gather | solution.py:89
  709.6 22.4 convert_reduce_fusion
  732.1 22.1 convolution_bitcast_fusion
  754.2 238.2 %reduce-scatter.3.cloned.1.call-done = f32[256,2,2048]{0,2,1:T(8,128)} async-done(((f32[1024,2,2048]{0,2,1:T(8,128)}), f32[256,2,2048]{0,2,1:T(8,128)}) %reduce-scatter.3.cloned.1.call-update) | async-done | bytes 4194320 | tf_op jit(solution)/shard_map/reduce_scatter | solution.py:196
  992.3 4.0 convert_reduce_fusion.3
  996.8 1.9 convert_reduce_fusion.4
  1000.0 1.3 copy.87
  1001.3 2.3 copy.82
  1003.6 1.2 copy.103
  1004.9 2.3 copy.86
  1007.1 1.5 copy.85
  1008.6 26.3 fusion.13
  1034.9 65.5 %pad_maximum_fusion = f32[2048,12288]{1,0:T(8,128)} fusion(f32[2048,5120]{1,0:T(8,128)} %convolution_bitcast_fusion, f32[2048,7168]{1,0:T(8,128)} %fusion.13), kind=kLoop, calls=%fused_computation | loop fusion | flops 25165824 | bytes 201326592 | tf_op jit(solution)/shard_map/concatenate | solution.py:269
  1101.7 6.7 fusion.60
  1108.4 16.2 convolution_add_fusion
  1124.6 4.4 fusion.63
  1129.0 4.4 fusion.62
  1133.4 4.4 fusion.64
  1137.8 18.3 add_add_fusion
  1156.2 773.7 %reduce-scatter.5.cloned.1.call-done = f32[512,12288]{1,0:T(8,128)} async-done(((f32[2048,12288]{1,0:T(8,128)}), f32[512,12288]{1,0:T(8,128)}) %reduce-scatter.5.cloned.1.call-update) | async-done | bytes 25165840 | tf_op jit(solution)/shard_map/reduce_scatter | solution.py:268
  1930.6 2.0 convert_reduce_fusion.2
  1932.8 39.2 %all-reduce.7.cloned.1.call-done = (f32[512,2048]{1,0:T(8,128)}, f32[512,2048]{1,0:T(8,128)}) async-done(((f32[512,2048]{1,0:T(8,128)}, f32[512,2048]{1,0:T(8,128)}), (f32[512,2048]{1,0:T(8,128)}, f32[512,2048]{1,0:T(8,128)})) %all-reduce.7.cloned.1.call-update) | async-done | bytes 8388624 | tf_op jit(solution)/shard_map/psum | solution.py:153
  1972.0 3.6 fusion.38
  1975.7 82.3 %all-reduce = (f32[2048]{0:T(1024)}, f32[2048]{0:T(1024)}, f32[1024]{0:T(1024)}, f32[1024]{0:T(1024)}, f32[1024]{0:T(1024)}, /*index=5*/f32[4096]{0:T(1024)}, f32[2048]{0:T(1024)}) all-reduce(f32[2048]{0:T(1024)S(1)} %get-tuple-element.15, f32[2048]{0:T(1024)S(1)} %get-tuple-element.18, ...), channel_id=1, replica_groups=mesh['fsdp'=4,'ctx'=4,'tp'=2] {'fsdp','ctx'}, use_global_device_ids=true, to_apply=%region_13.14 | all-reduce | flops 13312 | bytes 106496 | tf_op jit(solution)/shard_map/psum | solution.py:252
  2058.0 6.8 fusion.37
  2064.8 745.8 %all-reduce.5.cloned.1.call-done = f32[512,12288]{1,0:T(8,128)} async-done(((f32[512,12288]{1,0:T(8,128)}), f32[512,12288]{1,0:T(8,128)}) %all-reduce.5.cloned.1.call-update) | async-done | bytes 25165840 | tf_op jit(solution)/shard_map/psum | solution.py:271
  2810.6 7.5 fusion.56
  2818.1 11.1 fusion.55
  (150 shorter events, 18.5 us)
Async XLA Ops:
  7.2 2.9 copy-start
  7.2 4.0 copy-start.34
  7.2 4.0 copy-start.30
  7.2 4.0 copy-start.31
  7.2 58.1 %all-gather.9.cloned.1.call-start = ((), (), s32[]{:S(2)}) async-start(), calls=%async_computation.2 | async-start | bytes 5242880 | tf_op jit(solution)/shard_map/all_gather | solution.py:86
  8.0 112.0 %all-gather.15.cloned.1.call-start = ((), (), s32[]{:S(2)}) async-start(), calls=%async_computation.5 | async-start | bytes 5242880 | tf_op jit(solution)/shard_map/all_gather | solution.py:85
  8.7 165.8 %all-gather.13.cloned.1.call-start = ((), (), s32[]{:S(2)}) async-start(), calls=%async_computation.4 | async-start | bytes 5242880 | tf_op jit(solution)/shard_map/all_gather | solution.py:84
  9.4 219.5 %all-gather.19.cloned.1.call-start = ((), (), s32[]{:S(2)}) async-start(), calls=%async_computation.7 | async-start | bytes 5242880 | tf_op jit(solution)/shard_map/all_gather | solution.py:87
  10.0 301.7 %all-gather.11.cloned.1.call-start = ((), (), s32[]{:S(2)}) async-start(), calls=%async_computation.3 | async-start | bytes 5242880 | tf_op jit(solution)/shard_map/all_gather | solution.py:126
  10.4 0.8 copy-start.21
  11.2 0.6 copy-start.23
  11.2 0.6 copy-start.18
  14.0 57.7 %copy-start.35 = (bf16[1024]{0:T(1024)(128)(2,1)S(1)}, bf16[1024]{0:T(1024)(128)(2,1)}, u32[]{:S(2)}) copy-start(bf16[1024]{0:T(1024)(128)(2,1)} %param.25) | copy-start | bytes 6148
  14.0 57.8 %copy-start.36 = (bf16[1024]{0:T(1024)(128)(2,1)S(1)}, bf16[1024]{0:T(1024)(128)(2,1)}, u32[]{:S(2)}) copy-start(bf16[1024]{0:T(1024)(128)(2,1)} %param.27) | copy-start | bytes 6148
  14.0 57.8 %copy-start.37 = (s32[8]{0:T(128)S(1)}, s32[8]{0:T(128)}, u32[]{:S(2)}) copy-start(s32[8]{0:T(128)} %param.21) | copy-start | bytes 100
  14.0 105.9 %copy-start.3 = (bf16[512,2048]{1,0:T(8,128)(2,1)S(1)}, bf16[512,2048]{1,0:T(8,128)(2,1)}, u32[]{:S(2)}) copy-start(bf16[512,2048]{1,0:T(8,128)(2,1)} %fusion.32) | copy-start | bytes 6291460
  71.5 321.4 %all-gather.17.cloned.1.call-start = ((), (), s32[]{:S(2)}) async-start(), calls=%async_computation.6 | async-start | bytes 5242880 | tf_op jit(solution)/shard_map/all_gather | solution.py:125
  72.7 128.0 %copy-start.16 = (f32[256,16]{0,1:T(8,128)}, f32[256,16]{0,1:T(8,128)S(1)}, u32[]{:S(2)}) copy-start(f32[256,16]{0,1:T(8,128)S(1)} %get-tuple-element.68) | copy-start | bytes 49156
  193.2 7.1 copy-start.5
  200.3 2.0 copy-start.15
  204.9 1.7 copy-start.38
  204.9 350.0 %all-gather.21.cloned.1.call-start = ((), (), s32[]{:S(2)}) async-start(), calls=%async_computation.8 | async-start | bytes 20971520 | tf_op jit(solution)/shard_map/all_gather | solution.py:88
  205.7 503.9 %all-gather.23.cloned.1.call-start = ((), (), s32[]{:S(2)}) async-start(), calls=%async_computation.9 | async-start | bytes 20971520 | tf_op jit(solution)/shard_map/all_gather | solution.py:89
  206.4 785.9 %reduce-scatter.3.cloned.1.call-start = ((), (), s32[]{:S(2)}) async-start(), calls=%async_computation.10 | async-start | bytes 20971520 | tf_op jit(solution)/shard_map/reduce_scatter | solution.py:196
  242.1 150.8 %copy-start.7 = (bf16[2,256,16,32]{1,3,2,0:T(8,128)(2,1)S(1)}, bf16[2,256,16,32]{1,3,2,0:T(8,128)(2,1)}, u32[]{:S(2)}) copy-start(bf16[2,256,16,32]{1,3,2,0:T(8,128)(2,1)} %copy.99) | copy-start | bytes 1572868
  242.1 150.8 %copy-start.8 = (pred[2,256,1024]{2,1,0:T(8,128)(4,1)S(1)}, pred[2,256,1024]{2,1,0:T(8,128)(4,1)}, u32[]{:S(2)}) copy-start(pred[2,256,1024]{2,1,0:T(8,128)(4,1)} %broadcast_or_fusion) | copy-start | bytes 1572868
  242.1 150.8 %copy-start.14 = (bf16[2,256,16,16]{1,3,2,0:T(8,128)(2,1)S(1)}, bf16[2,256,16,16]{1,3,2,0:T(8,128)(2,1)}, u32[]{:S(2)}) copy-start(bf16[2,256,16,16]{1,3,2,0:T(8,128)(2,1)} %get-tuple-element.57) | copy-start | bytes 786436
  412.9 14.6 copy-start.2
  520.5 0.7 copy-start.29
  520.5 1409.4 %reduce-scatter.5.cloned.1.call-start = ((), (), s32[]{:S(2)}) async-start(), calls=%async_computation.11 | async-start | bytes 125829120 | tf_op jit(solution)/shard_map/reduce_scatter | solution.py:268
  537.6 1.0 copy-start.9
  539.9 15.0 copy-start.4
  754.1 242.3 %copy-start.17 = (f32[256,16]{0,1:T(8,128)S(1)}, f32[256,16]{0,1:T(8,128)}, u32[]{:S(2)}) copy-start(f32[256,16]{0,1:T(8,128)} %copy-done.16) | copy-start | bytes 49156
  754.1 242.3 %copy-start.20 = (f32[256,16]{0,1:T(8,128)S(1)}, f32[256,16]{0,1:T(8,128)}, u32[]{:S(2)}) copy-start(f32[256,16]{0,1:T(8,128)} %get-tuple-element.66) | copy-start | bytes 49156
  992.3 4.1 copy-start.6
  1000.0 7.1 copy-start.11
  1100.5 1.2 copy-start.10
  1100.5 871.5 %all-reduce.7.cloned.1.call-start = ((), (), s32[]{:S(2)}) async-start(), calls=%async_computation.13 | async-start | bytes 16777216 | tf_op jit(solution)/shard_map/psum | solution.py:153
  1108.4 16.2 copy-start.12
  1108.4 16.2 copy-start.40
  1124.6 4.4 copy-start.13
  1124.6 4.4 copy-start.41
  1129.0 4.4 copy-start.39
  1156.2 1654.4 %all-reduce.5.cloned.1.call-start = ((), (), s32[]{:S(2)}) async-start(), calls=%async_computation.12 | async-start | bytes 50331648 | tf_op jit(solution)/shard_map/psum | solution.py:271
  1929.9 0.7 copy-start.32
  1929.9 0.7 copy-start.33
  1929.9 2.7 copy-start.26
  1929.9 2.8 copy-start.25
  1929.9 42.1 %copy-start.1 = (bf16[2,256,2048]{2,1,0:T(8,128)(2,1)S(1)}, bf16[2,256,2048]{2,1,0:T(8,128)(2,1)}, u32[]{:S(2)}) copy-start(bf16[2,256,2048]{2,1,0:T(8,128)(2,1)} %param.18) | copy-start | bytes 6291460
  1929.9 42.1 %copy-start.19 = (f32[2048]{0:T(1024)S(1)}, f32[2048]{0:T(1024)}, u32[]{:S(2)}) copy-start(f32[2048]{0:T(1024)} %copy-done.18) | copy-start | bytes 24580
  1929.9 42.1 %copy-start.22 = (f32[1,2,2,128]{3,1,2,0:T(2,128)S(1)}, f32[1,2,2,128]{3,1,2,0:T(2,128)}, u32[]{:S(2)}) copy-start(f32[1,2,2,128]{3,1,2,0:T(2,128)} %copy-done.21) | copy-start | bytes 6148
  1929.9 42.0 %copy-start.24 = (f32[1,2,2,128]{3,1,2,0:T(2,128)S(1)}, f32[1,2,2,128]{3,1,2,0:T(2,128)}, u32[]{:S(2)}) copy-start(f32[1,2,2,128]{3,1,2,0:T(2,128)} %copy-done.23) | copy-start | bytes 6148
  1930.6 45.0 %copy-start.27 = (f32[4096]{0:T(1024)S(1)}, f32[4096]{0:T(1024)}, u32[]{:S(2)}) copy-start(f32[4096]{0:T(1024)} %get-tuple-element.28) | copy-start | bytes 49156
  1930.6 45.0 %copy-start.28 = (f32[1024]{0:T(1024)S(1)}, f32[1024]{0:T(1024)}, u32[]{:S(2)}) copy-start(f32[1024]{0:T(1024)} %get-tuple-element.30) | copy-start | bytes 12292
Sparse Core Ops, SparseCore 0:
  9.9 55.3 all-gather.8
  67.2 52.6 all-gather.14
  121.8 52.6 all-gather.12
  176.2 52.6 all-gather.18
  230.9 80.7 all-gather.10
  313.7 79.0 all-gather.16
  394.7 155.5 all-gather.20
  552.2 157.4 all-gather.22
  712.0 280.2 reduce-scatter.2
  1100.6 829.2 reduce-scatter.4
  1933.0 38.8 all-reduce.6
  1974.3 836.1 all-reduce.4
where the time goes:
time: 2840 us
  waiting for transfers between devices  2240 us (79%)
  matrix products  263 us (9%)
  other arithmetic  148 us (5%)
  local copies, waits for them, and re-layouts  84.7 us (3%)
  blocking collectives  82.3 us (3%)
    reduce_scatter x1, waiting for transfers between devices, local(): lax.psum_scatter(jnp.concatenate([left_part, right_part], axis=1), 'fsdp'...  774 us
    psum x1, waiting for transfers between devices, local(): weight_grads = lax.psum(scattered, 'ctx')  746 us
    reduce_scatter x1, waiting for transfers between devices, local(): lax.psum_scatter(jnp.concatenate([grad_key_part.reshape(row_count, seq_co...  238 us
    all_gather x1, waiting for transfers between devices, local(): lax.all_gather(down_weight, 'fsdp', axis=0, tiled=True)  140 us
    psum x1, blocking collectives, local(): lax.psum((small_terms[0], small_terms[1], small_terms[2], small_terms[3],...  82.3 us
    all_gather x1, waiting for transfers between devices, local(): lax.all_gather(key_rot, 'ctx', axis=1, tiled=True)  74.9 us
    all_gather x1, waiting for transfers between devices, local(): lax.all_gather(value_rows, 'ctx', axis=1, tiled=True)  69.7 us
    concatenate x1, other arithmetic, local(): jnp.concatenate([left_part, right_part], axis=1)  65.5 us
  transfers between devices with their start and end apart: 12, of which 11 were waited for; matrix products, arithmetic and copies ran while one was open for 13% of the time, Pallas kernels for 0%

commit v1 on v0

--- a/solution.py
+++ b/solution.py
@@ -8,6 +8,28 @@
 SEQ_LEN = 1024
 masked_fill = -1e30
 norm_eps = 1e-05
+
+
+def in_order(pieces, dim):
+    lengths = list(pieces.shape[1:])
+    lengths[dim] *= pieces.shape[0]
+    return jnp.moveaxis(pieces, 0, dim).reshape(lengths)
+
+
+def gather_around(x, axis, dim):
+    length = lax.axis_size(axis)
+    pairs = [(i, (i + 1) % length) for i in range(length)]
+    back = [(b, a) for a, b in pairs]
+    lower, upper = ([], [])
+    for step in range(length - 1):
+        if step % 2 == 0:
+            lower.append(lax.ppermute(lower[-1] if lower else x, axis, pairs))
+        else:
+            upper.append(lax.ppermute(upper[-1] if upper else x, axis, back))
+    blocks = jnp.stack([*lower[::-1], x, *upper])
+    shift = lax.axis_index(axis) - len(lower)
+    blocks = blocks[(jnp.arange(length) - shift) % length]
+    return in_order(blocks, dim)
 
 
 def positions(group_order, row_start, row_count, group_len):
@@ -123,7 +145,7 @@
     )
     keys_all, values_all = (
         lax.all_gather(key_rot, "ctx", axis=1, tiled=True),
-        lax.all_gather(value_rows, "ctx", axis=1, tiled=True),
+        gather_around(value_rows, "ctx", 1),
     )
 
     def scores_for(key_block):

time: 2840 us -> 2840 us (level)
  waiting for transfers between devices: 2240 us -> 2210 us
    all_gather x1, waiting for transfers between devices: 140 us -> 41.6 us  [local(): lax.all_gather(down_weight, 'fsdp', axis=0, tiled=True)]
    ppermute x0 -> x3, waiting for transfers between devices: none -> 68.2 us  [the longest x2 48.5 us: gather_around(): lower.append(lax.ppermute(lower[-1] if lower else x, axis, pairs))]
  transfers between devices with their start and end apart: 12 -> 15, of which waited for: 11 -> 14; matrix products, arithmetic and copies ran while one was open for 13% -> 14% of each run, Pallas kernels for 0% -> 0%
where the time goes in v1:
time: 2840 us
  waiting for transfers between devices  2210 us (78%)
  matrix products  265 us (9%)
  other arithmetic  152 us (5%)
  local copies, waits for them, and re-layouts  105 us (4%)
  blocking collectives  82.3 us (3%)
    reduce_scatter x1, waiting for transfers between devices, local(): lax.psum_scatter(jnp.concatenate([left_part, right_part], axis=1), 'fsdp'...  774 us
    psum x1, waiting for transfers between devices, local(): weight_grads = lax.psum(scattered, 'ctx')  746 us
    reduce_scatter x1, waiting for transfers between devices, local(): lax.psum_scatter(jnp.concatenate([grad_key_part.reshape(row_count, seq_co...  238 us
    psum x1, blocking collectives, local(): lax.psum((small_terms[0], small_terms[1], small_terms[2], small_terms[3],...  82.3 us
    all_gather x1, waiting for transfers between devices, local(): lax.all_gather(key_rot, 'ctx', axis=1, tiled=True)  74.9 us
    all_gather x1, waiting for transfers between devices, local(): lax.all_gather(value_rows, 'ctx', axis=1, tiled=True)  69.7 us
    concatenate x1, other arithmetic, local(): jnp.concatenate([left_part, right_part], axis=1)  65.5 us
  transfers between devices with their start and end apart: 15, of which 14 were waited for; matrix products, arithmetic and copies ran while one was open for 14% of the time, Pallas kernels for 0%

profile of v1, /device:TPU:0, one launch (start us, length us, event | category | flops | bytes accessed | tf_op | source)
XLA Modules:
  0.0 2836.2 jit_solution(17949404115226587864)
XLA Ops:
  11.8 2.2 fusion.32
  14.0 51.3 %all-gather.9.cloned.1.call-done = bf16[2048,1024]{1,0:T(8,128)(2,1)} async-done(((bf16[512,1024]{1,0:T(8,128)(2,1)}), bf16[2048,1024]{1,0:T(8,128)(2,1)}) %all-gather.9.cloned.1.call-update) | async-done | bytes 4194320 | tf_op jit(solution)/shard_map/all_gather | solution.py:108
  65.3 6.1 add_convert_fusion
  72.7 47.3 %all-gather.13.cloned.1.call-done = bf16[2048,1024]{1,0:T(8,128)(2,1)} async-done(((bf16[512,1024]{1,0:T(8,128)(2,1)}), bf16[2048,1024]{1,0:T(8,128)(2,1)}) %all-gather.13.cloned.1.call-update) | async-done | bytes 4194320 | tf_op jit(solution)/shard_map/all_gather | solution.py:107
  119.9 5.8 convolution_add_fusion.1
  125.8 2.9 copy.75
  128.6 3.7 reshape.435
  132.3 2.5 slice.116
  134.8 39.8 %all-gather.11.cloned.1.call-done = bf16[2048,1024]{1,0:T(8,128)(2,1)} async-done(((bf16[512,1024]{1,0:T(8,128)(2,1)}), bf16[2048,1024]{1,0:T(8,128)(2,1)}) %all-gather.11.cloned.1.call-update) | async-done | bytes 4194320 | tf_op jit(solution)/shard_map/all_gather | solution.py:106
  174.5 5.8 convolution_add_fusion.2
  180.3 4.5 reshape.455
  184.9 8.3 fusion.59
  193.2 3.6 copy.101
  196.8 3.5 copy.100
  207.9 2.8 slice.87
  210.7 18.2 all-gather.17.cloned.1.call-done
  228.9 5.2 convolution_convert_fusion
  234.1 2.7 reshape.456
  236.8 2.9 copy.84
  239.7 2.4 copy.102
  242.1 69.7 %all-gather.23.cloned.1.call-done = bf16[2,1024,1024]{2,1,0:T(8,128)(2,1)} async-done(((bf16[2,256,1024]{2,1,0:T(8,128)(2,1)}), bf16[2,1024,1024]{2,1,0:T(8,128)(2,1)}) %all-gather.23.cloned.1.call-update) | async-done | bytes 4194320 | tf_op jit(solution)/shard_map/all_gather | solution.py:188
  311.7 6.2 copy.83
  317.9 74.9 %all-gather.15.cloned.1.call-done = bf16[2,1024,1024]{1,2,0:T(8,128)(2,1)} async-done(((bf16[2,256,1024]{1,2,0:T(8,128)(2,1)}), bf16[2,1024,1024]{1,2,0:T(8,128)(2,1)}) %all-gather.15.cloned.1.call-update) | async-done | bytes 4194320 | tf_op jit(solution)/shard_map/all_gather | solution.py:147
  392.9 20.1 fusion.61
  412.9 14.6 fusion
  427.5 22.3 multiply_reduce_fusion
  449.8 29.6 %multiply_convert_fusion = bf16[2,16,256,1024]{3,2,1,0:T(8,128)(2,1)} fusion(f32[2,16,256,1024]{3,2,1,0:T(8,128)} %get-tuple-element.72, f32[2,16,256,1024]{3,2,1,0:T(8,128)} %get-tuple-element.70, f32[2,16,256]{2,1,0:T(8,128)S(1)} %get-tuple-element.71, f32[2,16,256]{2,1,0:T(8,128)S(1)} %log_add_fusion), kind=kLoop, calls=%fused_computation.2 | loop fusion | flops 33554432 | bytes 83951616 | tf_op jit(solution)/shard_map/convert_element_type | solution.py:202
  479.4 12.2 broadcast_multiply_fusion
  491.6 17.0 fusion.2
  508.6 11.9 pad_maximum_fusion.1
  521.7 3.8 collective-permute-start.2
  525.5 24.0 collective-permute-done
  549.6 19.7 collective-permute-done.2
  569.3 24.4 collective-permute-done.1
  593.7 3.3 pad_maximum_fusion.2
  597.1 5.0 gather_fusion
  602.1 7.5 copy.70
  609.6 7.7 reshape_reshape.3
  617.3 17.4 fusion.43
  638.3 13.7 multiply_bitcast_fusion
  653.4 14.6 fusion.63
  668.0 41.6 %all-gather.21.cloned.1.call-done = bf16[2048,4096]{1,0:T(8,128)(2,1)} async-done(((bf16[512,4096]{1,0:T(8,128)(2,1)}), bf16[2048,4096]{1,0:T(8,128)(2,1)}) %all-gather.21.cloned.1.call-update) | async-done | bytes 16777232 | tf_op jit(solution)/shard_map/all_gather | solution.py:111
  709.6 22.0 convert_reduce_fusion
  731.7 22.3 convolution_bitcast_fusion
  754.0 238.3 %reduce-scatter.3.cloned.1.call-done = f32[256,2,2048]{0,2,1:T(8,128)} async-done(((f32[1024,2,2048]{0,2,1:T(8,128)}), f32[256,2,2048]{0,2,1:T(8,128)}) %reduce-scatter.3.cloned.1.call-update) | async-done | bytes 4194320 | tf_op jit(solution)/shard_map/reduce_scatter | solution.py:218
  992.3 4.0 convert_reduce_fusion.3
  1001.3 2.3 copy.85
  1004.9 2.3 copy.89
  1008.6 26.2 fusion.13
  1034.8 65.5 %pad_maximum_fusion = f32[2048,12288]{1,0:T(8,128)} fusion(f32[2048,5120]{1,0:T(8,128)} %convolution_bitcast_fusion, f32[2048,7168]{1,0:T(8,128)} %fusion.13), kind=kLoop, calls=%fused_computation.1 | loop fusion | flops 25165824 | bytes 201326592 | tf_op jit(solution)/shard_map/concatenate | solution.py:291
  1101.6 6.7 fusion.62
  1108.3 16.2 convolution_add_fusion
  1124.5 4.4 fusion.65
  1128.9 4.4 fusion.64
  1133.3 4.4 fusion.66
  1137.7 18.3 add_add_fusion
  1156.1 773.8 %reduce-scatter.5.cloned.1.call-done = f32[512,12288]{1,0:T(8,128)} async-done(((f32[2048,12288]{1,0:T(8,128)}), f32[512,12288]{1,0:T(8,128)}) %reduce-scatter.5.cloned.1.call-update) | async-done | bytes 25165840 | tf_op jit(solution)/shard_map/reduce_scatter | solution.py:290
  1932.8 39.2 %all-reduce.7.cloned.1.call-done = (f32[512,2048]{1,0:T(8,128)}, f32[512,2048]{1,0:T(8,128)}) async-done(((f32[512,2048]{1,0:T(8,128)}, f32[512,2048]{1,0:T(8,128)}), (f32[512,2048]{1,0:T(8,128)}, f32[512,2048]{1,0:T(8,128)})) %all-reduce.7.cloned.1.call-update) | async-done | bytes 8388624 | tf_op jit(solution)/shard_map/psum | solution.py:175
  1972.0 3.6 fusion.38
  1975.6 82.3 %all-reduce = (f32[2048]{0:T(1024)}, f32[2048]{0:T(1024)}, f32[1024]{0:T(1024)}, f32[1024]{0:T(1024)}, f32[1024]{0:T(1024)}, /*index=5*/f32[4096]{0:T(1024)}, f32[2048]{0:T(1024)}) all-reduce(f32[2048]{0:T(1024)S(1)} %get-tuple-element.15, f32[2048]{0:T(1024)S(1)} %get-tuple-element.18, ...), channel_id=1, replica_groups=mesh['fsdp'=4,'ctx'=4,'tp'=2] {'fsdp','ctx'}, use_global_device_ids=true, to_apply=%region_13.14 | all-reduce | flops 13312 | bytes 106496 | tf_op jit(solution)/shard_map/psum | solution.py:274
  2058.0 6.8 fusion.37
  2064.7 745.8 %all-reduce.5.cloned.1.call-done = f32[512,12288]{1,0:T(8,128)} async-done(((f32[512,12288]{1,0:T(8,128)}), f32[512,12288]{1,0:T(8,128)}) %all-reduce.5.cloned.1.call-update) | async-done | bytes 25165840 | tf_op jit(solution)/shard_map/psum | solution.py:293
  2810.6 7.5 fusion.58
  2818.1 11.1 fusion.57
  (164 shorter events, 31.0 us)
Async XLA Ops:
  7.2 2.9 copy-start
  7.2 4.0 copy-start.35
  7.2 4.0 copy-start.31
  7.2 4.0 copy-start.32
  7.2 58.1 %all-gather.9.cloned.1.call-start = ((), (), s32[]{:S(2)}) async-start(), calls=%async_computation.2 | async-start | bytes 5242880 | tf_op jit(solution)/shard_map/all_gather | solution.py:108
  8.0 112.0 %all-gather.13.cloned.1.call-start = ((), (), s32[]{:S(2)}) async-start(), calls=%async_computation.4 | async-start | bytes 5242880 | tf_op jit(solution)/shard_map/all_gather | solution.py:107
  8.7 165.8 %all-gather.11.cloned.1.call-start = ((), (), s32[]{:S(2)}) async-start(), calls=%async_computation.3 | async-start | bytes 5242880 | tf_op jit(solution)/shard_map/all_gather | solution.py:106
  9.4 219.5 %all-gather.17.cloned.1.call-start = ((), (), s32[]{:S(2)}) async-start(), calls=%async_computation.6 | async-start | bytes 5242880 | tf_op jit(solution)/shard_map/all_gather | solution.py:109
  10.0 301.7 %all-gather.23.cloned.1.call-start = ((), (), s32[]{:S(2)}) async-start(), calls=%async_computation.9 | async-start | bytes 5242880 | tf_op jit(solution)/shard_map/all_gather | solution.py:188
  10.4 0.8 copy-start.22
  11.2 0.6 copy-start.24
  11.2 0.6 copy-start.19
  14.0 57.7 %copy-start.36 = (bf16[1024]{0:T(1024)(128)(2,1)S(1)}, bf16[1024]{0:T(1024)(128)(2,1)}, u32[]{:S(2)}) copy-start(bf16[1024]{0:T(1024)(128)(2,1)} %param.25) | copy-start | bytes 6148
  14.0 57.8 %copy-start.37 = (bf16[1024]{0:T(1024)(128)(2,1)S(1)}, bf16[1024]{0:T(1024)(128)(2,1)}, u32[]{:S(2)}) copy-start(bf16[1024]{0:T(1024)(128)(2,1)} %param.27) | copy-start | bytes 6148
  14.0 57.8 %copy-start.38 = (s32[8]{0:T(128)S(1)}, s32[8]{0:T(128)}, u32[]{:S(2)}) copy-start(s32[8]{0:T(128)} %param.21) | copy-start | bytes 100
  14.0 105.9 %copy-start.3 = (bf16[512,2048]{1,0:T(8,128)(2,1)S(1)}, bf16[512,2048]{1,0:T(8,128)(2,1)}, u32[]{:S(2)}) copy-start(bf16[512,2048]{1,0:T(8,128)(2,1)} %fusion.32) | copy-start | bytes 6291460
  71.5 321.4 %all-gather.15.cloned.1.call-start = ((), (), s32[]{:S(2)}) async-start(), calls=%async_computation.5 | async-start | bytes 5242880 | tf_op jit(solution)/shard_map/all_gather | solution.py:147
  72.7 128.0 %copy-start.17 = (f32[256,16]{0,1:T(8,128)}, f32[256,16]{0,1:T(8,128)S(1)}, u32[]{:S(2)}) copy-start(f32[256,16]{0,1:T(8,128)S(1)} %get-tuple-element.68) | copy-start | bytes 49156
  193.2 7.1 copy-start.5
  200.3 2.0 copy-start.16
  204.9 1.7 copy-start.39
  204.9 448.4 %all-gather.19.cloned.1.call-start = ((), (), s32[]{:S(2)}) async-start(), calls=%async_computation.7 | async-start | bytes 20971520 | tf_op jit(solution)/shard_map/all_gather | solution.py:110
  205.7 503.9 %all-gather.21.cloned.1.call-start = ((), (), s32[]{:S(2)}) async-start(), calls=%async_computation.8 | async-start | bytes 20971520 | tf_op jit(solution)/shard_map/all_gather | solution.py:111
  206.4 785.9 %reduce-scatter.3.cloned.1.call-start = ((), (), s32[]{:S(2)}) async-start(), calls=%async_computation.10 | async-start | bytes 20971520 | tf_op jit(solution)/shard_map/reduce_scatter | solution.py:218
  242.1 150.8 %copy-start.7 = (bf16[2,256,16,32]{1,3,2,0:T(8,128)(2,1)S(1)}, bf16[2,256,16,32]{1,3,2,0:T(8,128)(2,1)}, u32[]{:S(2)}) copy-start(bf16[2,256,16,32]{1,3,2,0:T(8,128)(2,1)} %copy.102) | copy-start | bytes 1572868
  242.1 150.8 %copy-start.8 = (pred[2,256,1024]{2,1,0:T(8,128)(4,1)S(1)}, pred[2,256,1024]{2,1,0:T(8,128)(4,1)}, u32[]{:S(2)}) copy-start(pred[2,256,1024]{2,1,0:T(8,128)(4,1)} %broadcast_or_fusion) | copy-start | bytes 1572868
  242.1 150.8 %copy-start.15 = (bf16[2,256,16,16]{1,3,2,0:T(8,128)(2,1)S(1)}, bf16[2,256,16,16]{1,3,2,0:T(8,128)(2,1)}, u32[]{:S(2)}) copy-start(bf16[2,256,16,16]{1,3,2,0:T(8,128)(2,1)} %get-tuple-element.57) | copy-start | bytes 786436
  412.9 14.6 copy-start.2
  520.5 1.2 copy-start.14
  520.5 29.1 %copy-start.30 = (bf16[4096]{0:T(1024)(128)(2,1)S(1)}, bf16[4096]{0:T(1024)(128)(2,1)}, u32[]{:S(2)}) copy-start(bf16[4096]{0:T(1024)(128)(2,1)} %param.33) | copy-start | bytes 24580
  520.5 1409.4 %reduce-scatter.5.cloned.1.call-start = ((), (), s32[]{:S(2)}) async-start(), calls=%async_computation.11 | async-start | bytes 125829120 | tf_op jit(solution)/shard_map/reduce_scatter | solution.py:290
  521.7 27.9 collective-permute-start
  521.7 47.6 %collective-permute-start.2 = (bf16[2,256,1024]{2,1,0:T(8,128)(2,1)S(1)}, bf16[2,256,1024]{2,1,0:T(8,128)(2,1)S(1)}, u32[]{:S(2)}, u32[]{:S(2)}) collective-permute-start(bf16[2,256,1024]{2,1,0:T(8,128)(2,1)S(1)} %bitcast.149), channel_id=1, source_target_pairs={{2,0},{4,2},{6,4},{0,6},{3,1},{5,3},{7,5},{1,7},{10,8},{12,10},{14... | collective-permute-start | bytes 3145736 | tf_op jit(solution)/shard_map/ppermute | solution.py:28
  549.5 44.2 %collective-permute-start.1 = (bf16[2,256,1024]{2,1,0:T(8,128)(2,1)S(1)}, bf16[2,256,1024]{2,1,0:T(8,128)(2,1)}, u32[]{:S(2)}, u32[]{:S(2)}) collective-permute-start(bf16[2,256,1024]{2,1,0:T(8,128)(2,1)S(1)} %collective-permute-done), channel_id=1, source_target_pairs={{0,2},{2,4},{4,6},{6,0},{1,3},{3,5},{5,7},{7,1},{8,10},{10,12},{12... | collective-permute-start | bytes 3145736 | tf_op jit(solution)/shard_map/ppermute | solution.py:26
  636.0 1.0 copy-start.9
  638.3 15.0 copy-start.4
  754.0 242.5 %copy-start.18 = (f32[256,16]{0,1:T(8,128)S(1)}, f32[256,16]{0,1:T(8,128)}, u32[]{:S(2)}) copy-start(f32[256,16]{0,1:T(8,128)} %copy-done.17) | copy-start | bytes 49156
  754.0 242.5 %copy-start.21 = (f32[256,16]{0,1:T(8,128)S(1)}, f32[256,16]{0,1:T(8,128)}, u32[]{:S(2)}) copy-start(f32[256,16]{0,1:T(8,128)} %get-tuple-element.66) | copy-start | bytes 49156
  992.3 4.1 copy-start.6
  1000.0 7.1 copy-start.11
  1100.4 1.2 copy-start.10
  1100.4 871.6 %all-reduce.7.cloned.1.call-start = ((), (), s32[]{:S(2)}) async-start(), calls=%async_computation.13 | async-start | bytes 16777216 | tf_op jit(solution)/shard_map/psum | solution.py:175
  1108.3 16.2 copy-start.12
  1108.3 16.2 copy-start.41
  1124.5 4.4 copy-start.13
  1124.5 4.4 copy-start.42
  1128.9 4.4 copy-start.40
  1156.1 1654.5 %all-reduce.5.cloned.1.call-start = ((), (), s32[]{:S(2)}) async-start(), calls=%async_computation.12 | async-start | bytes 50331648 | tf_op jit(solution)/shard_map/psum | solution.py:293
  1929.9 0.7 copy-start.33
  1929.9 0.7 copy-start.34
  1929.9 2.7 copy-start.27
  1929.9 2.8 copy-start.26
  1929.9 42.1 %copy-start.1 = (bf16[2,256,2048]{2,1,0:T(8,128)(2,1)S(1)}, bf16[2,256,2048]{2,1,0:T(8,128)(2,1)}, u32[]{:S(2)}) copy-start(bf16[2,256,2048]{2,1,0:T(8,128)(2,1)} %param.18) | copy-start | bytes 6291460
  1929.9 42.0 %copy-start.20 = (f32[2048]{0:T(1024)S(1)}, f32[2048]{0:T(1024)}, u32[]{:S(2)}) copy-start(f32[2048]{0:T(1024)} %copy-done.19) | copy-start | bytes 24580
  1929.9 42.0 %copy-start.23 = (f32[1,2,2,128]{3,1,2,0:T(2,128)S(1)}, f32[1,2,2,128]{3,1,2,0:T(2,128)}, u32[]{:S(2)}) copy-start(f32[1,2,2,128]{3,1,2,0:T(2,128)} %copy-done.22) | copy-start | bytes 6148
  1929.9 42.0 %copy-start.25 = (f32[1,2,2,128]{3,1,2,0:T(2,128)S(1)}, f32[1,2,2,128]{3,1,2,0:T(2,128)}, u32[]{:S(2)}) copy-start(f32[1,2,2,128]{3,1,2,0:T(2,128)} %copy-done.24) | copy-start | bytes 6148
  1930.6 45.0 %copy-start.28 = (f32[4096]{0:T(1024)S(1)}, f32[4096]{0:T(1024)}, u32[]{:S(2)}) copy-start(f32[4096]{0:T(1024)} %get-tuple-element.28) | copy-start | bytes 49156
  1930.6 45.0 %copy-start.29 = (f32[1024]{0:T(1024)S(1)}, f32[1024]{0:T(1024)}, u32[]{:S(2)}) copy-start(f32[1024]{0:T(1024)} %get-tuple-element.30) | copy-start | bytes 12292
Sparse Core Ops, SparseCore 0:
  9.9 55.3 all-gather.8
  67.2 52.6 all-gather.12
  121.8 52.6 all-gather.10
  176.2 52.6 all-gather.16
  230.9 80.7 all-gather.22
  313.7 79.0 all-gather.14
  394.7 155.5 all-gather.18
  552.2 157.4 all-gather.20
  712.0 280.2 reduce-scatter.2
  1100.5 829.3 reduce-scatter.4
  1933.0 38.8 all-reduce.6
  1974.3 836.1 all-reduce.4
